TPU v7x, 512 devices: a whole 4x4x16 slice. The times are simulated.
512 devices in a mesh: region: 4 (over z_hi), dom: 128 (over x, y, z_lo, core).
Axes of the slice: x: 4, y: 4, z: 16 (z_hi: 4, z_lo: 4; z = z_hi * 4 + z_lo), core: 2. Of those that a mesh axis runs over, the one named last changes fastest.
Arguments:
- entity: float32 [400, 65536], P(None, 'dom'), may hold values from -3 to 3
- relation: float32 [400, 256], replicated, may hold values from -3.6 to 3.6
- head_index: int32 [262144], P(('region', 'dom')), may hold values from 0 to 511
- relation_index: int32 [262144], P(('region', 'dom')), may hold values from 0 to 255
- tail_index: int32 [262144], P(('region', 'dom')), may hold values from 0 to 511
- negative_index: int32 [589824], P(('region', 'dom')), may hold values from 0 to 511
- plan: int32 [1], replicated, may hold values from 1 to 127
- edge_count: int32 [512], P(('region', 'dom')), may hold values from 128 to 512, as said below
Outputs:
- entity_out: float32 [400, 65536], P(None, 'dom')
- relation_out: float32 [400, 256], replicated
Inputs may be any that keep to these rules, and one draw needn't show every extreme that they name: Dom index i is matched with index i XOR plan[0], its partner partition. A device's active edges are its first edge_count slots; in every draw some device uses all 512.
All inputs are finite; a program needn't handle non-finite values.
Results may differ from a plain program's by a relative error of at most 0.0032.
The roundings to bfloat16 on the way count: a program that leaves them out, or rounds other values in their place, can miss the bound.
Values may be sent and summed in bfloat16 or wider, within the bound.
A program may use at most 64 MiB of HBM per device.

v0:
```python
import functools

import jax
import jax.numpy as jnp
from jax import lax
from jax.experimental import pallas as pl
from jax.experimental.pallas import tpu as pltpu
from jax.sharding import PartitionSpec as P

entity_rate = 1.0
relation_rate = 0.1

F32 = jnp.float32
BF16 = jnp.bfloat16
MESH = pl.DeviceIdType.MESH


def move(value, offset):
    if offset == 0:
        return value
    pairs = [(source, source ^ offset) for source in range(lax.axis_size("dom"))]
    return lax.ppermute(value, "dom", pairs)


def route(payload, pattern):
    low = [functools.partial(move, offset=digit) for digit in range(8)]
    high = [functools.partial(move, offset=digit << 3) for digit in range(16)]
    payload = lax.switch(pattern & 7, low, payload)
    return lax.switch(pattern >> 3, high, payload)


def split(value, parts):
    pieces = []
    for _ in range(parts):
        piece = value.astype(BF16)
        pieces.append(piece)
        value = value - piece.astype(F32)
    return pieces


NN = (((1,), (0,)), ((), ()))
NT = (((1,), (1,)), ((), ()))
TN = (((0,), (0,)), ((), ()))


def matmul(pieces, other, dims):
    total = None
    for piece in pieces:
        part = lax.dot_general(piece, other, dims, preferred_element_type=F32)
        total = part if total is None else total + part
    return total


def one_hot(rows, index):
    shape = (rows, index.shape[1])
    return jnp.where(lax.broadcasted_iota(jnp.int32, shape, 0) == index, 1.0, 0.0).astype(BF16)


def terms_kernel(
    count_ref, entity_ref, relation_ref, partner_ref, head_ref, rel_ref, tail_ref, neg_ref,
    head_grad_ref, partner_grad_ref, rel_grad_ref, wide,
):
    features, block = entity_ref.shape
    half = features // 2
    rels = relation_ref.shape[1]
    edges = head_ref.shape[1]
    negatives = neg_ref.shape[1]
    count = count_ref[0]
    head_pick = one_hot(block, head_ref[...])
    rel_pick = one_hot(rels, rel_ref[...])
    tail_pick = one_hot(block, tail_ref[...])
    head = matmul(split(entity_ref[...], 3), head_pick, NN)
    rel = matmul(split(relation_ref[...], 3), rel_pick, NN)
    head_real, head_imag = head[:half], head[half:]
    rel_real, rel_imag = rel[:half], rel[half:]
    wide[:half, :] = head_real * rel_real - head_imag * rel_imag
    wide[half:, :] = head_real * rel_imag + head_imag * rel_real
    query = wide[...].astype(BF16)
    query_wide = query.astype(F32)
    neg_pick = one_hot(block, neg_ref[...])
    times = lax.dot_general(
        jnp.ones((8, negatives), BF16), neg_pick, NT, preferred_element_type=F32
    )[:1]

    partner = partner_ref[...]
    tail = lax.dot_general(partner, tail_pick, NN, preferred_element_type=F32)
    active = jnp.where(lax.broadcasted_iota(jnp.int32, (1, edges), 1) < count, 1.0, 0.0)
    positive = jnp.sum(query_wide * tail, axis=0, keepdims=True)
    positive_grad = -jax.nn.sigmoid(-positive) * active
    scores = lax.dot_general(query, partner, TN, preferred_element_type=F32)
    share = jnp.where(
        lax.broadcasted_iota(jnp.int32, (edges, 1), 0) < count, 1.0 / negatives, 0.0
    )
    weights = (jax.nn.sigmoid(scores) * share).astype(BF16).astype(F32) * times
    weight_hi, weight_lo = split(weights, 2)
    pull = (
        positive_grad * tail
        + lax.dot_general(partner, weight_hi, NT, preferred_element_type=F32)
        + lax.dot_general(partner, weight_lo, NT, preferred_element_type=F32)
    )
    partner_grad = (
        lax.dot_general(query, weight_hi, NN, preferred_element_type=F32)
        + lax.dot_general(query, weight_lo, NN, preferred_element_type=F32)
        + matmul(split(positive_grad * query_wide, 2), tail_pick, NT)
    )
    partner_grad_ref[...] = partner_grad.astype(BF16)
    pull_real, pull_imag = pull[:half], pull[half:]
    wide[:half, :] = pull_real * head_real + pull_imag * head_imag
    wide[half:, :] = pull_imag * head_real - pull_real * head_imag
    rel_grad_ref[:features, :] = matmul(split(wide[...], 2), rel_pick, NT)
    rel_grad_ref[features:, :] = jnp.zeros((rel_grad_ref.shape[0] - features, rels), F32)
    wide[:half, :] = pull_real * rel_real + pull_imag * rel_imag
    wide[half:, :] = pull_imag * rel_real - pull_real * rel_imag
    head_grad_ref[...] = matmul(split(wide[...], 2), head_pick, NT)


def edge_terms(edge_count, entity, relation, partner, head, rel, tail, neg):
    features, block = entity.shape
    vmem = pl.BlockSpec(memory_space=pltpu.VMEM)
    return pl.pallas_call(
        terms_kernel,
        out_shape=(
            jax.ShapeDtypeStruct((features, block), F32),
            jax.ShapeDtypeStruct((features, block), BF16),
            jax.ShapeDtypeStruct((512, relation.shape[1]), F32),
        ),
        in_specs=[pl.BlockSpec(memory_space=pltpu.SMEM)] + [vmem] * 7,
        out_specs=(vmem, vmem, vmem),
        scratch_shapes=[pltpu.VMEM((features, head.shape[1]), F32)],
        name="edge_terms",
    )(edge_count, entity, relation, partner, head, rel, tail, neg)


def sums_kernel(
    head_ref, returned_ref, rel_ref,
    entity_grad, relation_grad,
    mine, sent, far_up, far_down, both_up, both_down, got, shared,
    core_got, core_sum, x_got, x_sum, y_got, lo_all, hi_all, whole,
    send_sem, recv_sem,
):
    features, block = head_ref.shape
    quarter = block // 4
    region = lax.axis_index("region")
    dom = lax.axis_index("dom")
    x = dom // 32
    y = lax.rem(dom // 8, 4)
    z = lax.rem(dom // 2, 4)
    core = lax.rem(dom, 2)

    def at(region=region, x=x, y=y, z=z, core=core):
        return (region, ((x * 4 + y) * 4 + z) * 2 + core)

    def turn(value, step):
        return lax.rem(value + step, 4)

    def peer(axis, step):
        if axis == "core":
            return at(core=1 - core)
        if axis == "x":
            return at(x=turn(x, step))
        if axis == "y":
            return at(y=turn(y, step))
        if axis == "z":
            return at(z=turn(z, step))
        return at(region=turn(region, step))

    barrier = pltpu.get_barrier_semaphore()
    peers = [peer("core", 1)] + [peer(a, s) for a in ("x", "y", "z", "r") for s in (1, 2, 3)]
    for other in peers:
        pl.semaphore_signal(barrier, inc=1, device_id=other, device_id_type=MESH)

    for q in range(4):
        columns = slice(q * quarter, (q + 1) * quarter)
        value = head_ref[:, columns] + returned_ref[:, columns].astype(F32)
        mine[q] = value
        sent[q] = value.astype(BF16)

    pl.semaphore_wait(barrier, len(peers))
    used = [0]

    def send(src, dst, device):
        slot = used[0]
        used[0] += 1
        copy = pltpu.make_async_remote_copy(
            src_ref=src,
            dst_ref=dst,
            send_sem=send_sem.at[slot],
            recv_sem=recv_sem.at[slot],
            device_id=device,
            device_id_type=MESH,
        )
        copy.start()
        return copy

    def wait(copies):
        for copy in copies:
            copy.wait()

    steps = (2, 1, 3)
    up, down, far = turn(region, 1), turn(region, 3), turn(region, 2)
    above, below = peer("r", 1), peer("r", 3)
    cut = far_up.shape[0]
    top, low = pl.ds(0, cut), pl.ds(cut, features - cut)

    far_copies = [
        send(sent.at[far, top], far_up, above),
        send(sent.at[far, low], far_down, below),
    ]
    near_copies = [
        send(sent.at[up, low], got.at[0, low], above),
        send(sent.at[down, top], got.at[1, top], below),
    ]

    wait([send(rel_ref.at[1 - core], core_got, peer("core", 1))])
    core_sum[...] = rel_ref[core] + core_got[...]
    wait([send(core_sum.at[turn(x, s)], x_got.at[s - 1], peer("x", s)) for s in steps])
    x_sum[...] = core_sum[x] + x_got[0] + x_got[1] + x_got[2]
    y_copies = [send(x_sum.at[turn(y, s)], y_got.at[s - 1], peer("y", s)) for s in steps]

    wait(far_copies)
    both_up[...] = (mine[up, :cut] + far_up[...].astype(F32)).astype(BF16)
    both_down[...] = (mine[down, cut:] + far_down[...].astype(F32)).astype(BF16)
    near_copies += [
        send(both_up, got.at[0, top], above),
        send(both_down, got.at[1, low], below),
    ]

    wait(y_copies)
    lo_all[z] = x_sum[y] + y_got[0] + y_got[1] + y_got[2]
    wait([send(lo_all.at[z], lo_all.at[z], peer("z", s)) for s in steps])
    hi_all[region] = lo_all[0] + lo_all[1] + lo_all[2] + lo_all[3]
    hi_copies = [send(hi_all.at[region], hi_all.at[region], peer("r", s)) for s in steps]

    wait(near_copies)
    total = mine[region] + got[0].astype(F32) + got[1].astype(F32)
    shared[region] = total.astype(BF16)
    relayed = [
        send(shared.at[region, top], shared.at[region, top], above),
        send(shared.at[region, low], shared.at[region, low], below),
    ]
    last_copies = [
        send(shared.at[region, low], shared.at[region, low], above),
        send(shared.at[region, top], shared.at[region, top], below),
    ]

    wait(hi_copies)
    whole[core, x, y] = hi_all[0] + hi_all[1] + hi_all[2] + hi_all[3]
    y_copies = [send(whole.at[core, x, y], whole.at[core, x, y], peer("y", s)) for s in steps]
    wait(relayed)
    last_copies += [
        send(shared.at[down, top], shared.at[down, top], above),
        send(shared.at[up, low], shared.at[up, low], below),
    ]
    wait(y_copies)
    wait([send(whole.at[core, x], whole.at[core, x], peer("x", s)) for s in steps])
    wait([send(whole.at[core], whole.at[core], peer("core", 1))])
    for piece in range(features // 16):
        part = whole[piece // 16, piece // 4 % 4, piece % 4]
        relation_grad[piece * 16 : piece * 16 + 16, :] = part

    wait(last_copies)
    for q in range(4):
        entity_grad[:, q * quarter : (q + 1) * quarter] = shared[q]


def sum_all(head_grad, returned, rel_grad):
    features, block = head_grad.shape
    rels = rel_grad.shape[1]
    quarter = block // 4
    vmem = pl.BlockSpec(memory_space=pltpu.VMEM)
    piece = (16, rels)
    copies = 32
    cut = (features // 2 + 15) // 16 * 16
    return pl.pallas_call(
        sums_kernel,
        out_shape=(
            jax.ShapeDtypeStruct((features, block), BF16),
            jax.ShapeDtypeStruct((features, rels), F32),
        ),
        in_specs=[vmem] * 3,
        out_specs=(vmem, vmem),
        scratch_shapes=[
            pltpu.VMEM((4, features, quarter), F32),
            pltpu.VMEM((4, features, quarter), BF16),
            pltpu.VMEM((cut, quarter), BF16),
            pltpu.VMEM((features - cut, quarter), BF16),
            pltpu.VMEM((cut, quarter), BF16),
            pltpu.VMEM((features - cut, quarter), BF16),
            pltpu.VMEM((2, features, quarter), BF16),
            pltpu.VMEM((4, features, quarter), BF16),
            pltpu.VMEM((4, 4) + piece, F32),
            pltpu.VMEM((4, 4) + piece, F32),
            pltpu.VMEM((3, 4) + piece, F32),
            pltpu.VMEM((4,) + piece, F32),
            pltpu.VMEM((3,) + piece, F32),
            pltpu.VMEM((4,) + piece, F32),
            pltpu.VMEM((4,) + piece, F32),
            pltpu.VMEM((2, 4, 4) + piece, F32),
            pltpu.SemaphoreType.DMA((copies,)),
            pltpu.SemaphoreType.DMA((copies,)),
        ],
        compiler_params=pltpu.CompilerParams(collective_id=0, has_side_effects=True),
        name="sum_all",
    )(head_grad, returned, rel_grad.reshape((2, 4, 4) + piece))


def shards(
    entity, relation, head_index, relation_index, tail_index, negative_index, plan, edge_count
):
    pattern = plan[0]
    partner = route(entity.astype(BF16), pattern)
    head_grad, partner_grad, rel_grad = edge_terms(
        edge_count,
        entity,
        relation,
        partner,
        head_index[None, :],
        relation_index[None, :],
        tail_index[None, :],
        negative_index[None, :],
    )
    returned = route(partner_grad, pattern)
    entity_grad, relation_grad = sum_all(head_grad, returned, rel_grad)
    return entity - entity_rate * entity_grad.astype(F32), relation - relation_rate * relation_grad


def solution(mesh):
    in_specs = (
        P(None, "dom"),
        P(),
        P(("region", "dom")),
        P(("region", "dom")),
        P(("region", "dom")),
        P(("region", "dom")),
        P(),
        P(("region", "dom")),
    )
    out_specs = (P(None, "dom"), P())
    return jax.shard_map(shards, mesh=mesh, in_specs=in_specs, out_specs=out_specs, check_vma=False)
```

profile of v0, /device:TPU:1, one launch (start us, length us, event | category | flops | bytes accessed | tf_op | source)
XLA Modules:
  0.0 130.3 jit_solution(1680569845684235849)
XLA Ops:
  1.9 0.0 copy-start.3
  1.9 0.7 copy-done.3
  2.6 0.6 broadcast_in_dim.15.neg_ref
  3.2 1.2 convert_element_type.30
  4.4 14.6 %conditional.4 = (bf16[400,512]{1,0:T(8,128)(2,1)S(1)}) conditional(s32[]{:T(128)} %bitcast.1, bf16[400,512]{1,0:T(8,128)(2,1)S(1)} %convert_element_type.30, bf16[400,512]{1,0:T(8,128)(2,1)S(1)} %convert_element_type.30, bf16[400,512]{1,0:T(8,128)(2,1)S(1)} %convert_element_type.30, ...), branch_computations={%region_0.0_spmd, %region_1.0_spmd, %region_2.0_spmd, %region_3.0_... | conditional | bytes 2457648 | solution.py:28
  4.5 7.1 %collective-permute-start.5 = (bf16[400,512]{1,0:T(8,128)(2,1)S(1)}, bf16[400,512]{1,0:T(8,128)(2,1)S(1)}, u32[]{:S(2)}, u32[]{:S(2)}) collective-permute-start(bf16[400,512]{1,0:T(8,128)(2,1)S(1)} %param.6), channel_id=1, source_target_pairs={{0,6},{1,7},{2,4},{3,5},{4,2},{5,3},{6,0},{7,1},{8,14},{9,15},{10,... | collective-permute-start | bytes 1228808 | tf_op jit(solution)/shard_map/cond/branch_6_fun/ppermute | solution.py:22
  11.5 7.5 %collective-permute-done.5 = bf16[400,512]{1,0:T(8,128)(2,1)S(1)} collective-permute-done((bf16[400,512]{1,0:T(8,128)(2,1)S(1)}, bf16[400,512]{1,0:T(8,128)(2,1)S(1)}, u32[]{:S(2)}, u32[]{:S(2)}) %collective-permute-start.5) | collective-permute-done | bytes 409632 | tf_op jit(solution)/shard_map/cond/branch_6_fun/ppermute | solution.py:22
  19.1 13.4 %conditional.5 = (bf16[400,512]{1,0:T(8,128)(2,1)S(1)}) conditional(s32[]{:T(128)} %bitcast, bf16[400,512]{1,0:T(8,128)(2,1)S(1)} %get-tuple-element.112, bf16[400,512]{1,0:T(8,128)(2,1)S(1)} %get-tuple-element.112, bf16[400,512]{1,0:T(8,128)(2,1)S(1)} %get-tuple-element.112, ...), branch_computations={%region_8.0_spmd, %region_9.0_spmd, %region_10.0_spmd, %region_11.... | conditional | bytes 2457648 | solution.py:29
  19.1 5.8 %collective-permute-start.11 = (bf16[400,512]{1,0:T(8,128)(2,1)S(1)}, bf16[400,512]{1,0:T(8,128)(2,1)S(1)}, u32[]{:S(2)}, u32[]{:S(2)}) collective-permute-start(bf16[400,512]{1,0:T(8,128)(2,1)S(1)} %param.13), channel_id=1, source_target_pairs={{0,40},{1,41},{2,42},{3,43},{4,44},{5,45},{6,46},{7,47},{8,32},{9,... | collective-permute-start | bytes 1228808 | tf_op jit(solution)/shard_map/cond/branch_5_fun/ppermute | solution.py:22
  25.0 7.5 %collective-permute-done.11 = bf16[400,512]{1,0:T(8,128)(2,1)S(1)} collective-permute-done((bf16[400,512]{1,0:T(8,128)(2,1)S(1)}, bf16[400,512]{1,0:T(8,128)(2,1)S(1)}, u32[]{:S(2)}, u32[]{:S(2)}) %collective-permute-start.11) | collective-permute-done | bytes 409632 | tf_op jit(solution)/shard_map/cond/branch_5_fun/ppermute | solution.py:22
  32.5 6.7 %edge_terms.1 = (f32[400,512]{1,0:T(8,128)}, bf16[400,512]{1,0:T(8,128)(2,1)S(1)}, f32[512,256]{1,0:T(8,128)}) custom-call(s32[1]{0:T(128)S(6)} %copy.59.count_ref, f32[400,512]{1,0:T(8,128)} %entity_ref.1, f32[400,256]{1,0:T(8,128)} %relation_ref.1, bf16[400,512]{1,0:T(8,128)(2,1)S(1)} %get-tuple-element.113.partner_ref, s32[1,512]{1,0:T(1,128)} %bitcast.7, ...), custom_call_target="tpu_custom_call" | custom-call | tf_op jit(solution)/shard_map/edge_terms/pallas_call | solution.py:120
  39.2 12.1 %conditional.6 = (bf16[400,512]{1,0:T(8,128)(2,1)S(1)}) conditional(s32[]{:T(128)} %bitcast.1, bf16[400,512]{1,0:T(8,128)(2,1)S(1)} %get-tuple-element.108, bf16[400,512]{1,0:T(8,128)(2,1)S(1)} %get-tuple-element.108, bf16[400,512]{1,0:T(8,128)(2,1)S(1)} %get-tuple-element.108, ...), branch_computations={%region_24.0_spmd, %region_25.0_spmd, %region_26.0_spmd, %region_2... | conditional | bytes 2457648 | solution.py:28
  39.2 5.3 %collective-permute-start.27 = (bf16[400,512]{1,0:T(8,128)(2,1)S(1)}, bf16[400,512]{1,0:T(8,128)(2,1)S(1)}, u32[]{:S(2)}, u32[]{:S(2)}) collective-permute-start(bf16[400,512]{1,0:T(8,128)(2,1)S(1)} %param.30), channel_id=1, source_target_pairs={{0,6},{1,7},{2,4},{3,5},{4,2},{5,3},{6,0},{7,1},{8,14},{9,15},{10,... | collective-permute-start | bytes 1228808 | tf_op jit(solution)/shard_map/cond/branch_6_fun/ppermute | solution.py:22
  44.5 6.8 %collective-permute-done.27 = bf16[400,512]{1,0:T(8,128)(2,1)S(1)} collective-permute-done((bf16[400,512]{1,0:T(8,128)(2,1)S(1)}, bf16[400,512]{1,0:T(8,128)(2,1)S(1)}, u32[]{:S(2)}, u32[]{:S(2)}) %collective-permute-start.27) | collective-permute-done | bytes 409632 | tf_op jit(solution)/shard_map/cond/branch_6_fun/ppermute | solution.py:22
  51.4 12.3 %conditional.7 = (bf16[400,512]{1,0:T(8,128)(2,1)S(1)}) conditional(s32[]{:T(128)} %bitcast, bf16[400,512]{1,0:T(8,128)(2,1)S(1)} %get-tuple-element.114, bf16[400,512]{1,0:T(8,128)(2,1)S(1)} %get-tuple-element.114, bf16[400,512]{1,0:T(8,128)(2,1)S(1)} %get-tuple-element.114, ...), branch_computations={%region_32.0_spmd, %region_33.0_spmd, %region_34.0_spmd, %region_3... | conditional | bytes 2457648 | solution.py:29
  51.4 5.5 %collective-permute-start.33 = (bf16[400,512]{1,0:T(8,128)(2,1)S(1)}, bf16[400,512]{1,0:T(8,128)(2,1)S(1)}, u32[]{:S(2)}, u32[]{:S(2)}) collective-permute-start(bf16[400,512]{1,0:T(8,128)(2,1)S(1)} %param.37), channel_id=1, source_target_pairs={{0,40},{1,41},{2,42},{3,43},{4,44},{5,45},{6,46},{7,47},{8,32},{9,... | collective-permute-start | bytes 1228808 | tf_op jit(solution)/shard_map/cond/branch_5_fun/ppermute | solution.py:22
  56.9 6.7 %collective-permute-done.33 = bf16[400,512]{1,0:T(8,128)(2,1)S(1)} collective-permute-done((bf16[400,512]{1,0:T(8,128)(2,1)S(1)}, bf16[400,512]{1,0:T(8,128)(2,1)S(1)}, u32[]{:S(2)}, u32[]{:S(2)}) %collective-permute-start.33) | collective-permute-done | bytes 409632 | tf_op jit(solution)/shard_map/cond/branch_5_fun/ppermute | solution.py:22
  63.7 0.0 copy-start
  63.7 63.7 %sum_all.1 = (bf16[400,512]{1,0:T(8,128)(2,1)}, f32[400,256]{1,0:T(8,128)}) custom-call(f32[400,512]{1,0:T(8,128)} %get-tuple-element.107.head_ref, bf16[400,512]{1,0:T(8,128)(2,1)S(1)} %get-tuple-element.115.returned_ref, f32[2,4,4,16,256]{4,3,2,1,0:T(8,128)} %bitcast.6), custom_call_target="tpu_custom_call" | custom-call | tf_op jit(solution)/shard_map/sum_all/pallas_call | solution.py:274
  127.4 0.0 copy-done
  127.4 0.0 copy-start.1
  127.4 0.0 copy-start.2
  127.4 2.1 %convert_subtract_fusion = f32[400,512]{1,0:T(8,128)} fusion(f32[400,512]{1,0:T(8,128)S(1)} %copy-done, bf16[400,512]{1,0:T(8,128)(2,1)} %get-tuple-element.110), kind=kLoop, calls=%fused_computation | loop fusion | flops 409600 | bytes 2048000 | tf_op jit(solution)/shard_map/sub | solution.py:324
  129.5 0.8 multiply_subtract_fusion
  (6 shorter events, 0.1 us)
Async XLA Ops:
  1.9 0.7 copy-start.3
  4.5 14.6 %collective-permute-start.5 = (bf16[400,512]{1,0:T(8,128)(2,1)S(1)}, bf16[400,512]{1,0:T(8,128)(2,1)S(1)}, u32[]{:S(2)}, u32[]{:S(2)}) collective-permute-start(bf16[400,512]{1,0:T(8,128)(2,1)S(1)} %param.6), channel_id=1, source_target_pairs={{0,6},{1,7},{2,4},{3,5},{4,2},{5,3},{6,0},{7,1},{8,14},{9,15},{10,... | collective-permute-start | bytes 1228808 | tf_op jit(solution)/shard_map/cond/branch_6_fun/ppermute | solution.py:22
  19.1 13.4 %collective-permute-start.11 = (bf16[400,512]{1,0:T(8,128)(2,1)S(1)}, bf16[400,512]{1,0:T(8,128)(2,1)S(1)}, u32[]{:S(2)}, u32[]{:S(2)}) collective-permute-start(bf16[400,512]{1,0:T(8,128)(2,1)S(1)} %param.13), channel_id=1, source_target_pairs={{0,40},{1,41},{2,42},{3,43},{4,44},{5,45},{6,46},{7,47},{8,32},{9,... | collective-permute-start | bytes 1228808 | tf_op jit(solution)/shard_map/cond/branch_5_fun/ppermute | solution.py:22
  39.2 12.1 %collective-permute-start.27 = (bf16[400,512]{1,0:T(8,128)(2,1)S(1)}, bf16[400,512]{1,0:T(8,128)(2,1)S(1)}, u32[]{:S(2)}, u32[]{:S(2)}) collective-permute-start(bf16[400,512]{1,0:T(8,128)(2,1)S(1)} %param.30), channel_id=1, source_target_pairs={{0,6},{1,7},{2,4},{3,5},{4,2},{5,3},{6,0},{7,1},{8,14},{9,15},{10,... | collective-permute-start | bytes 1228808 | tf_op jit(solution)/shard_map/cond/branch_6_fun/ppermute | solution.py:22
  51.4 12.2 %collective-permute-start.33 = (bf16[400,512]{1,0:T(8,128)(2,1)S(1)}, bf16[400,512]{1,0:T(8,128)(2,1)S(1)}, u32[]{:S(2)}, u32[]{:S(2)}) collective-permute-start(bf16[400,512]{1,0:T(8,128)(2,1)S(1)} %param.37), channel_id=1, source_target_pairs={{0,40},{1,41},{2,42},{3,43},{4,44},{5,45},{6,46},{7,47},{8,32},{9,... | collective-permute-start | bytes 1228808 | tf_op jit(solution)/shard_map/cond/branch_5_fun/ppermute | solution.py:22
  63.7 63.8 %copy-start = (f32[400,512]{1,0:T(8,128)S(1)}, f32[400,512]{1,0:T(8,128)}, u32[]{:S(2)}) copy-start(f32[400,512]{1,0:T(8,128)} %entity_ref.1) | copy-start | bytes 2457604
  127.4 2.1 %copy-start.1 = (f32[400,256]{1,0:T(8,128)S(1)}, f32[400,256]{1,0:T(8,128)}, u32[]{:S(2)}) copy-start(f32[400,256]{1,0:T(8,128)} %relation_ref.1) | copy-start | bytes 1228804
  127.4 2.1 %copy-start.2 = (f32[400,256]{1,0:T(8,128)S(1)}, f32[400,256]{1,0:T(8,128)}, u32[]{:S(2)}) copy-start(f32[400,256]{1,0:T(8,128)} %get-tuple-element.111) | copy-start | bytes 1228804
where the time goes:
time: 132 us; the launch traced here: 130 us
  Pallas kernels  70.5 us (53%)
  waiting for transfers between devices  28.5 us (22%)
  starting transfers between devices  23.7 us (18%)
  other arithmetic  4.08 us (3%)
  between operations  2.01 us (2%)
  local copies, waits for them, and re-layouts  1.41 us (1%)
    pallas_call x1, Pallas kernels, sum_all(): pl.pallas_call(sums_kernel, out_shape=(jax.ShapeDtypeStruct((features, bl...  63.7 us
    ppermute x4, waiting for transfers between devices, move(): return lax.ppermute(value, 'dom', pairs)  28.5 us
    ppermute x4, starting transfers between devices, move(): return lax.ppermute(value, 'dom', pairs)  23.7 us
    pallas_call x1, Pallas kernels, edge_terms(): pl.pallas_call(terms_kernel, out_shape=(jax.ShapeDtypeStruct((features, b...  6.74 us
  transfers between devices with their start and end apart: 4, of which 4 were waited for; matrix products, arithmetic and copies ran while one was open for 0% of the time, Pallas kernels for 0%

commit v1 on v0

--- a/solution.py
+++ b/solution.py
@@ -18,8 +18,17 @@
 def move(value, offset):
     if offset == 0:
         return value
-    pairs = [(source, source ^ offset) for source in range(lax.axis_size("dom"))]
-    return lax.ppermute(value, "dom", pairs)
+    regions = lax.axis_size("region")
+    count = lax.axis_size("dom")
+    z_offset = offset >> 1 & 3
+    pairs = []
+    for region in range(regions):
+        for source in range(count):
+            z = source >> 1 & 3
+            turn = {0: -1, 3: 1}.get(z, 0) if z_offset > 1 else 0
+            target = (region + turn) % regions * count + (source ^ offset)
+            pairs.append((region * count + source, target))
+    return lax.ppermute(value, ("region", "dom"), pairs)
 
 
 def route(payload, pattern):
@@ -64,7 +73,7 @@
     half = features // 2
     rels = relation_ref.shape[1]
     edges = head_ref.shape[1]
-    negatives = neg_ref.shape[1]
+    negatives = neg_ref.shape[0]
     count = count_ref[0]
     head_pick = one_hot(block, head_ref[...])
     rel_pick = one_hot(rels, rel_ref[...])
@@ -77,7 +86,7 @@
     wide[half:, :] = head_real * rel_imag + head_imag * rel_real
     query = wide[...].astype(BF16)
     query_wide = query.astype(F32)
-    neg_pick = one_hot(block, neg_ref[...])
+    neg_pick = one_hot(block, neg_ref[...].reshape(1, negatives))
     times = lax.dot_general(
         jnp.ones((8, negatives), BF16), neg_pick, NT, preferred_element_type=F32
     )[:1]
@@ -135,7 +144,7 @@
     head_ref, returned_ref, rel_ref,
     entity_grad, relation_grad,
     mine, sent, far_up, far_down, both_up, both_down, got, shared,
-    core_got, core_sum, x_got, x_sum, y_got, lo_all, hi_all, whole,
+    core_got, core_sum, x_got, x_sum, y_got, lo_all, pair_mine, pair_got, whole,
     send_sem, recv_sem,
 ):
     features, block = head_ref.shape
@@ -165,7 +174,8 @@
         return at(region=turn(region, step))
 
     barrier = pltpu.get_barrier_semaphore()
-    peers = [peer("core", 1)] + [peer(a, s) for a in ("x", "y", "z", "r") for s in (1, 2, 3)]
+    peers = [peer("core", 1), peer("r", 1), peer("r", 3)]
+    peers += [peer(a, s) for a in ("x", "y", "z") for s in (1, 2, 3)]
     for other in peers:
         pl.semaphore_signal(barrier, inc=1, device_id=other, device_id_type=MESH)
 
@@ -199,6 +209,8 @@
     steps = (2, 1, 3)
     up, down, far = turn(region, 1), turn(region, 3), turn(region, 2)
     above, below = peer("r", 1), peer("r", 3)
+    first = at(region=region + 1 - 2 * lax.rem(region, 2))
+    second = at(region=3 - region)
     cut = far_up.shape[0]
     top, low = pl.ds(0, cut), pl.ds(cut, features - cut)
 
@@ -228,8 +240,8 @@
     wait(y_copies)
     lo_all[z] = x_sum[y] + y_got[0] + y_got[1] + y_got[2]
     wait([send(lo_all.at[z], lo_all.at[z], peer("z", s)) for s in steps])
-    hi_all[region] = lo_all[0] + lo_all[1] + lo_all[2] + lo_all[3]
-    hi_copies = [send(hi_all.at[region], hi_all.at[region], peer("r", s)) for s in steps]
+    pair_mine[0] = lo_all[0] + lo_all[1] + lo_all[2] + lo_all[3]
+    pair_copies = [send(pair_mine.at[0], pair_got.at[0], first)]
 
     wait(near_copies)
     total = mine[region] + got[0].astype(F32) + got[1].astype(F32)
@@ -243,15 +255,17 @@
         send(shared.at[region, top], shared.at[region, top], below),
     ]
 
-    wait(hi_copies)
-    whole[core, x, y] = hi_all[0] + hi_all[1] + hi_all[2] + hi_all[3]
-    y_copies = [send(whole.at[core, x, y], whole.at[core, x, y], peer("y", s)) for s in steps]
+    wait(pair_copies)
+    pair_mine[1] = pair_mine[0] + pair_got[0]
+    pair_copies = [send(pair_mine.at[1], pair_got.at[1], second)]
     wait(relayed)
     last_copies += [
         send(shared.at[down, top], shared.at[down, top], above),
         send(shared.at[up, low], shared.at[up, low], below),
     ]
-    wait(y_copies)
+    wait(pair_copies)
+    whole[core, x, y] = pair_mine[1] + pair_got[1]
+    wait([send(whole.at[core, x, y], whole.at[core, x, y], peer("y", s)) for s in steps])
     wait([send(whole.at[core, x], whole.at[core, x], peer("x", s)) for s in steps])
     wait([send(whole.at[core], whole.at[core], peer("core", 1))])
     for piece in range(features // 16):
@@ -269,7 +283,7 @@
     quarter = block // 4
     vmem = pl.BlockSpec(memory_space=pltpu.VMEM)
     piece = (16, rels)
-    copies = 32
+    copies = 31
     cut = (features // 2 + 15) // 16 * 16
     return pl.pallas_call(
         sums_kernel,
@@ -294,7 +308,8 @@
             pltpu.VMEM((4,) + piece, F32),
             pltpu.VMEM((3,) + piece, F32),
             pltpu.VMEM((4,) + piece, F32),
-            pltpu.VMEM((4,) + piece, F32),
+            pltpu.VMEM((2,) + piece, F32),
+            pltpu.VMEM((2,) + piece, F32),
             pltpu.VMEM((2, 4, 4) + piece, F32),
             pltpu.SemaphoreType.DMA((copies,)),
             pltpu.SemaphoreType.DMA((copies,)),
@@ -317,7 +332,7 @@
         head_index[None, :],
         relation_index[None, :],
         tail_index[None, :],
-        negative_index[None, :],
+        negative_index,
     )
     returned = route(partner_grad, pattern)
     entity_grad, relation_grad = sum_all(head_grad, returned, rel_grad)

time: 132 us -> 133 us (level)
  Pallas kernels: 70.5 us -> 60.2 us
  waiting for transfers between devices: 28.5 us -> 37.7 us
  starting transfers between devices: 23.7 us -> 28.3 us
    pallas_call x1, Pallas kernels: 63.7 us -> 53.5 us  [sum_all(): pl.pallas_call(sums_kernel, out_shape=(jax.ShapeDtypeStruct((features, bl...]
    ppermute x4, waiting for transfers between devices: 28.5 us -> 37.7 us  [move(): return lax.ppermute(value, ('region', 'dom'), pairs)]
    ppermute x4, starting transfers between devices: 23.7 us -> 28.3 us  [move(): return lax.ppermute(value, ('region', 'dom'), pairs)]
where the time goes in v1:
time: 133 us
  Pallas kernels  60.2 us (45%)
  waiting for transfers between devices  37.7 us (28%)
  starting transfers between devices  28.3 us (21%)
  other arithmetic  4.08 us (3%)
  between operations  2 us (2%)
    pallas_call x1, Pallas kernels, sum_all(): pl.pallas_call(sums_kernel, out_shape=(jax.ShapeDtypeStruct((features, bl...  53.5 us
    ppermute x4, waiting for transfers between devices, move(): return lax.ppermute(value, ('region', 'dom'), pairs)  37.7 us
    ppermute x4, starting transfers between devices, move(): return lax.ppermute(value, ('region', 'dom'), pairs)  28.3 us
    pallas_call x1, Pallas kernels, edge_terms(): pl.pallas_call(terms_kernel, out_shape=(jax.ShapeDtypeStruct((features, b...  6.74 us
  transfers between devices with their start and end apart: 4, of which 4 were waited for; matrix products, arithmetic and copies ran while one was open for 0% of the time, Pallas kernels for 0%

profile of v1, /device:TPU:1, one launch (start us, length us, event | category | flops | bytes accessed | tf_op | source)
XLA Modules:
  0.0 132.5 jit_solution(2399721506120687484)
XLA Ops:
  1.9 1.2 convert_element_type.30
  3.1 21.8 %conditional.4 = (bf16[400,512]{1,0:T(8,128)(2,1)S(1)}) conditional(s32[]{:T(128)} %bitcast.1, bf16[400,512]{1,0:T(8,128)(2,1)S(1)} %convert_element_type.30, bf16[400,512]{1,0:T(8,128)(2,1)S(1)} %convert_element_type.30, bf16[400,512]{1,0:T(8,128)(2,1)S(1)} %convert_element_type.30, ...), branch_computations={%region_0.0_spmd, %region_1.0_spmd, %region_2.0_spmd, %region_3.0_... | conditional | bytes 2457648 | solution.py:37
  3.2 12.5 %collective-permute-start.6 = (bf16[400,512]{1,0:T(8,128)(2,1)S(1)}, bf16[400,512]{1,0:T(8,128)(2,1)S(1)}, u32[]{:S(2)}, u32[]{:S(2)}) collective-permute-start(bf16[400,512]{1,0:T(8,128)(2,1)S(1)} %param.7), channel_id=1, source_target_pairs={{0,391},{1,390},{2,5},{3,4},{4,3},{5,2},{6,129},{7,128},{8,399},{9... | collective-permute-start | bytes 1228808 | tf_op jit(solution)/shard_map/cond/branch_7_fun/ppermute | solution.py:31
  15.7 9.2 %collective-permute-done.6 = bf16[400,512]{1,0:T(8,128)(2,1)S(1)} collective-permute-done((bf16[400,512]{1,0:T(8,128)(2,1)S(1)}, bf16[400,512]{1,0:T(8,128)(2,1)S(1)}, u32[]{:S(2)}, u32[]{:S(2)}) %collective-permute-start.6) | collective-permute-done | bytes 409632 | tf_op jit(solution)/shard_map/cond/branch_7_fun/ppermute | solution.py:31
  25.0 14.1 %conditional.5 = (bf16[400,512]{1,0:T(8,128)(2,1)S(1)}) conditional(s32[]{:T(128)} %bitcast, bf16[400,512]{1,0:T(8,128)(2,1)S(1)} %get-tuple-element.112, bf16[400,512]{1,0:T(8,128)(2,1)S(1)} %get-tuple-element.112, bf16[400,512]{1,0:T(8,128)(2,1)S(1)} %get-tuple-element.112, ...), branch_computations={%region_8.0_spmd, %region_9.0_spmd, %region_10.0_spmd, %region_11.... | conditional | bytes 2457648 | solution.py:38
  25.0 4.7 %collective-permute-start.14 = (bf16[400,512]{1,0:T(8,128)(2,1)S(1)}, bf16[400,512]{1,0:T(8,128)(2,1)S(1)}, u32[]{:S(2)}, u32[]{:S(2)}) collective-permute-start(bf16[400,512]{1,0:T(8,128)(2,1)S(1)} %param.16), channel_id=1, source_target_pairs={{0,64},{1,65},{2,66},{3,67},{4,68},{5,69},{6,70},{7,71},{8,72},{9,... | collective-permute-start | bytes 1228808 | tf_op jit(solution)/shard_map/cond/branch_8_fun/ppermute | solution.py:31
  29.7 9.3 %collective-permute-done.14 = bf16[400,512]{1,0:T(8,128)(2,1)S(1)} collective-permute-done((bf16[400,512]{1,0:T(8,128)(2,1)S(1)}, bf16[400,512]{1,0:T(8,128)(2,1)S(1)}, u32[]{:S(2)}, u32[]{:S(2)}) %collective-permute-start.14) | collective-permute-done | bytes 409632 | tf_op jit(solution)/shard_map/cond/branch_8_fun/ppermute | solution.py:31
  39.1 6.7 %edge_terms.1 = (f32[400,512]{1,0:T(8,128)}, bf16[400,512]{1,0:T(8,128)(2,1)S(1)}, f32[512,256]{1,0:T(8,128)}) custom-call(s32[1]{0:T(128)S(6)} %copy.59.count_ref, f32[400,512]{1,0:T(8,128)} %entity_ref.1, f32[400,256]{1,0:T(8,128)} %relation_ref.1, bf16[400,512]{1,0:T(8,128)(2,1)S(1)} %get-tuple-element.113.partner_ref, s32[1,512]{1,0:T(1,128)} %bitcast.7, ...), custom_call_target="tpu_custom_call" | custom-call | tf_op jit(solution)/shard_map/edge_terms/pallas_call | solution.py:129
  45.8 15.5 %conditional.6 = (bf16[400,512]{1,0:T(8,128)(2,1)S(1)}) conditional(s32[]{:T(128)} %bitcast.1, bf16[400,512]{1,0:T(8,128)(2,1)S(1)} %get-tuple-element.108, bf16[400,512]{1,0:T(8,128)(2,1)S(1)} %get-tuple-element.108, bf16[400,512]{1,0:T(8,128)(2,1)S(1)} %get-tuple-element.108, ...), branch_computations={%region_24.0_spmd, %region_25.0_spmd, %region_26.0_spmd, %region_2... | conditional | bytes 2457648 | solution.py:37
  45.8 6.5 %collective-permute-start.28 = (bf16[400,512]{1,0:T(8,128)(2,1)S(1)}, bf16[400,512]{1,0:T(8,128)(2,1)S(1)}, u32[]{:S(2)}, u32[]{:S(2)}) collective-permute-start(bf16[400,512]{1,0:T(8,128)(2,1)S(1)} %param.31), channel_id=1, source_target_pairs={{0,391},{1,390},{2,5},{3,4},{4,3},{5,2},{6,129},{7,128},{8,399},{9... | collective-permute-start | bytes 1228808 | tf_op jit(solution)/shard_map/cond/branch_7_fun/ppermute | solution.py:31
  52.3 9.0 %collective-permute-done.28 = bf16[400,512]{1,0:T(8,128)(2,1)S(1)} collective-permute-done((bf16[400,512]{1,0:T(8,128)(2,1)S(1)}, bf16[400,512]{1,0:T(8,128)(2,1)S(1)}, u32[]{:S(2)}, u32[]{:S(2)}) %collective-permute-start.28) | collective-permute-done | bytes 409632 | tf_op jit(solution)/shard_map/cond/branch_7_fun/ppermute | solution.py:31
  61.3 14.9 %conditional.7 = (bf16[400,512]{1,0:T(8,128)(2,1)S(1)}) conditional(s32[]{:T(128)} %bitcast, bf16[400,512]{1,0:T(8,128)(2,1)S(1)} %get-tuple-element.114, bf16[400,512]{1,0:T(8,128)(2,1)S(1)} %get-tuple-element.114, bf16[400,512]{1,0:T(8,128)(2,1)S(1)} %get-tuple-element.114, ...), branch_computations={%region_32.0_spmd, %region_33.0_spmd, %region_34.0_spmd, %region_3... | conditional | bytes 2457648 | solution.py:38
  61.3 4.7 %collective-permute-start.36 = (bf16[400,512]{1,0:T(8,128)(2,1)S(1)}, bf16[400,512]{1,0:T(8,128)(2,1)S(1)}, u32[]{:S(2)}, u32[]{:S(2)}) collective-permute-start(bf16[400,512]{1,0:T(8,128)(2,1)S(1)} %param.40), channel_id=1, source_target_pairs={{0,64},{1,65},{2,66},{3,67},{4,68},{5,69},{6,70},{7,71},{8,72},{9,... | collective-permute-start | bytes 1228808 | tf_op jit(solution)/shard_map/cond/branch_8_fun/ppermute | solution.py:31
  66.0 10.1 %collective-permute-done.36 = bf16[400,512]{1,0:T(8,128)(2,1)S(1)} collective-permute-done((bf16[400,512]{1,0:T(8,128)(2,1)S(1)}, bf16[400,512]{1,0:T(8,128)(2,1)S(1)}, u32[]{:S(2)}, u32[]{:S(2)}) %collective-permute-start.36) | collective-permute-done | bytes 409632 | tf_op jit(solution)/shard_map/cond/branch_8_fun/ppermute | solution.py:31
  76.2 0.0 copy-start
  76.2 53.5 %sum_all.1 = (bf16[400,512]{1,0:T(8,128)(2,1)}, f32[400,256]{1,0:T(8,128)}) custom-call(f32[400,512]{1,0:T(8,128)} %get-tuple-element.107.head_ref, bf16[400,512]{1,0:T(8,128)(2,1)S(1)} %get-tuple-element.115.returned_ref, f32[2,4,4,16,256]{4,3,2,1,0:T(8,128)} %bitcast.6), custom_call_target="tpu_custom_call" | custom-call | tf_op jit(solution)/shard_map/sum_all/pallas_call | solution.py:288
  129.6 0.0 copy-done
  129.6 0.0 copy-start.1
  129.6 0.0 copy-start.2
  129.7 2.1 %convert_subtract_fusion = f32[400,512]{1,0:T(8,128)} fusion(f32[400,512]{1,0:T(8,128)S(1)} %copy-done, bf16[400,512]{1,0:T(8,128)(2,1)} %get-tuple-element.110), kind=kLoop, calls=%fused_computation | loop fusion | flops 409600 | bytes 2048000 | tf_op jit(solution)/shard_map/sub | solution.py:339
  131.7 0.0 copy-done.1
  131.7 0.0 copy-done.2
  131.7 0.8 multiply_subtract_fusion
  (4 shorter events, 0.1 us)
Async XLA Ops:
  3.2 21.8 %collective-permute-start.6 = (bf16[400,512]{1,0:T(8,128)(2,1)S(1)}, bf16[400,512]{1,0:T(8,128)(2,1)S(1)}, u32[]{:S(2)}, u32[]{:S(2)}) collective-permute-start(bf16[400,512]{1,0:T(8,128)(2,1)S(1)} %param.7), channel_id=1, source_target_pairs={{0,391},{1,390},{2,5},{3,4},{4,3},{5,2},{6,129},{7,128},{8,399},{9... | collective-permute-start | bytes 1228808 | tf_op jit(solution)/shard_map/cond/branch_7_fun/ppermute | solution.py:31
  25.0 14.0 %collective-permute-start.14 = (bf16[400,512]{1,0:T(8,128)(2,1)S(1)}, bf16[400,512]{1,0:T(8,128)(2,1)S(1)}, u32[]{:S(2)}, u32[]{:S(2)}) collective-permute-start(bf16[400,512]{1,0:T(8,128)(2,1)S(1)} %param.16), channel_id=1, source_target_pairs={{0,64},{1,65},{2,66},{3,67},{4,68},{5,69},{6,70},{7,71},{8,72},{9,... | collective-permute-start | bytes 1228808 | tf_op jit(solution)/shard_map/cond/branch_8_fun/ppermute | solution.py:31
  45.8 15.5 %collective-permute-start.28 = (bf16[400,512]{1,0:T(8,128)(2,1)S(1)}, bf16[400,512]{1,0:T(8,128)(2,1)S(1)}, u32[]{:S(2)}, u32[]{:S(2)}) collective-permute-start(bf16[400,512]{1,0:T(8,128)(2,1)S(1)} %param.31), channel_id=1, source_target_pairs={{0,391},{1,390},{2,5},{3,4},{4,3},{5,2},{6,129},{7,128},{8,399},{9... | collective-permute-start | bytes 1228808 | tf_op jit(solution)/shard_map/cond/branch_7_fun/ppermute | solution.py:31
  61.3 14.8 %collective-permute-start.36 = (bf16[400,512]{1,0:T(8,128)(2,1)S(1)}, bf16[400,512]{1,0:T(8,128)(2,1)S(1)}, u32[]{:S(2)}, u32[]{:S(2)}) collective-permute-start(bf16[400,512]{1,0:T(8,128)(2,1)S(1)} %param.40), channel_id=1, source_target_pairs={{0,64},{1,65},{2,66},{3,67},{4,68},{5,69},{6,70},{7,71},{8,72},{9,... | collective-permute-start | bytes 1228808 | tf_op jit(solution)/shard_map/cond/branch_8_fun/ppermute | solution.py:31
  76.2 53.5 %copy-start = (f32[400,512]{1,0:T(8,128)S(1)}, f32[400,512]{1,0:T(8,128)}, u32[]{:S(2)}) copy-start(f32[400,512]{1,0:T(8,128)} %entity_ref.1) | copy-start | bytes 2457604
  129.6 2.1 %copy-start.1 = (f32[400,256]{1,0:T(8,128)S(1)}, f32[400,256]{1,0:T(8,128)}, u32[]{:S(2)}) copy-start(f32[400,256]{1,0:T(8,128)} %relation_ref.1) | copy-start | bytes 1228804
  129.6 2.1 %copy-start.2 = (f32[400,256]{1,0:T(8,128)S(1)}, f32[400,256]{1,0:T(8,128)}, u32[]{:S(2)}) copy-start(f32[400,256]{1,0:T(8,128)} %get-tuple-element.111) | copy-start | bytes 1228804

commit v2 on v1

--- a/solution.py
+++ b/solution.py
@@ -36,6 +36,19 @@
     high = [functools.partial(move, offset=digit << 3) for digit in range(16)]
     payload = lax.switch(pattern & 7, low, payload)
     return lax.switch(pattern >> 3, high, payload)
+
+
+def route_beside(payload, rel_grad, pattern):
+    def low(digit, value, rel):
+        return move(value, digit), scatter_sum(rel)
+
+    def high(digit, value, rel):
+        return move(value, digit << 3), along_sum(rel)
+
+    lows = [functools.partial(low, digit) for digit in range(8)]
+    highs = [functools.partial(high, digit) for digit in range(16)]
+    payload, piece = lax.switch(pattern & 7, lows, payload, rel_grad)
+    return lax.switch(pattern >> 3, highs, payload, piece)
 
 
 def split(value, parts):
@@ -140,15 +153,7 @@
     )(edge_count, entity, relation, partner, head, rel, tail, neg)
 
 
-def sums_kernel(
-    head_ref, returned_ref, rel_ref,
-    entity_grad, relation_grad,
-    mine, sent, far_up, far_down, both_up, both_down, got, shared,
-    core_got, core_sum, x_got, x_sum, y_got, lo_all, pair_mine, pair_got, whole,
-    send_sem, recv_sem,
-):
-    features, block = head_ref.shape
-    quarter = block // 4
+def position():
     region = lax.axis_index("region")
     dom = lax.axis_index("dom")
     x = dom // 32
@@ -171,21 +176,22 @@
             return at(y=turn(y, step))
         if axis == "z":
             return at(z=turn(z, step))
+        if axis == "pair":
+            other = region + 1 - 2 * lax.rem(region, 2) if step == 1 else 3 - region
+            return at(region=other)
         return at(region=turn(region, step))
 
+    return region, x, y, z, core, peer, turn
+
+
+def greet(peers):
     barrier = pltpu.get_barrier_semaphore()
-    peers = [peer("core", 1), peer("r", 1), peer("r", 3)]
-    peers += [peer(a, s) for a in ("x", "y", "z") for s in (1, 2, 3)]
     for other in peers:
         pl.semaphore_signal(barrier, inc=1, device_id=other, device_id_type=MESH)
-
-    for q in range(4):
-        columns = slice(q * quarter, (q + 1) * quarter)
-        value = head_ref[:, columns] + returned_ref[:, columns].astype(F32)
-        mine[q] = value
-        sent[q] = value.astype(BF16)
-
-    pl.semaphore_wait(barrier, len(peers))
+    return lambda: pl.semaphore_wait(barrier, len(peers))
+
+
+def sender(send_sem, recv_sem):
     used = [0]
 
     def send(src, dst, device):
@@ -202,32 +208,108 @@
         copy.start()
         return copy
 
-    def wait(copies):
-        for copy in copies:
-            copy.wait()
-
+    return send
+
+
+def wait(copies):
+    for copy in copies:
+        copy.wait()
+
+
+def scatter_kernel(
+    rel_ref, piece_ref, core_got, core_sum, x_got, x_sum, y_got, send_sem, recv_sem
+):
+    region, x, y, z, core, peer, turn = position()
     steps = (2, 1, 3)
-    up, down, far = turn(region, 1), turn(region, 3), turn(region, 2)
-    above, below = peer("r", 1), peer("r", 3)
-    first = at(region=region + 1 - 2 * lax.rem(region, 2))
-    second = at(region=3 - region)
-    cut = far_up.shape[0]
-    top, low = pl.ds(0, cut), pl.ds(cut, features - cut)
-
-    far_copies = [
-        send(sent.at[far, top], far_up, above),
-        send(sent.at[far, low], far_down, below),
-    ]
-    near_copies = [
-        send(sent.at[up, low], got.at[0, low], above),
-        send(sent.at[down, top], got.at[1, top], below),
-    ]
-
+    greet([peer("core", 1)] + [peer(a, s) for a in ("x", "y") for s in steps])()
+    send = sender(send_sem, recv_sem)
     wait([send(rel_ref.at[1 - core], core_got, peer("core", 1))])
     core_sum[...] = rel_ref[core] + core_got[...]
     wait([send(core_sum.at[turn(x, s)], x_got.at[s - 1], peer("x", s)) for s in steps])
     x_sum[...] = core_sum[x] + x_got[0] + x_got[1] + x_got[2]
-    y_copies = [send(x_sum.at[turn(y, s)], y_got.at[s - 1], peer("y", s)) for s in steps]
+    wait([send(x_sum.at[turn(y, s)], y_got.at[s - 1], peer("y", s)) for s in steps])
+    piece_ref[...] = x_sum[y] + y_got[0] + y_got[1] + y_got[2]
+
+
+def along_kernel(piece_ref, sum_ref, lo_all, pair_mine, pair_got, send_sem, recv_sem):
+    region, x, y, z, core, peer, turn = position()
+    steps = (2, 1, 3)
+    greet([peer("z", s) for s in steps] + [peer("r", 1), peer("r", 3)])()
+    send = sender(send_sem, recv_sem)
+    lo_all[z] = piece_ref[...]
+    wait([send(lo_all.at[z], lo_all.at[z], peer("z", s)) for s in steps])
+    pair_mine[0] = lo_all[0] + lo_all[1] + lo_all[2] + lo_all[3]
+    wait([send(pair_mine.at[0], pair_got.at[0], peer("pair", 1))])
+    pair_mine[1] = pair_mine[0] + pair_got[0]
+    wait([send(pair_mine.at[1], pair_got.at[1], peer("pair", 2))])
+    sum_ref[...] = pair_mine[1] + pair_got[1]
+
+
+def small_sum(kernel, value, scratch, copies, number, name):
+    piece = (16, value.shape[-1])
+    vmem = pl.BlockSpec(memory_space=pltpu.VMEM)
+    return pl.pallas_call(
+        kernel,
+        out_shape=jax.ShapeDtypeStruct(piece, F32),
+        in_specs=[vmem],
+        out_specs=vmem,
+        scratch_shapes=[pltpu.VMEM(shape + piece, F32) for shape in scratch]
+        + [pltpu.SemaphoreType.DMA((copies,))] * 2,
+        compiler_params=pltpu.CompilerParams(collective_id=number, has_side_effects=True),
+        cost_estimate=pl.CostEstimate(flops=10**7, bytes_accessed=10**7, transcendentals=0),
+        name=name,
+    )(value)
+
+
+def scatter_sum(rel_grad):
+    value = rel_grad.reshape((2, 4, 4, 16, rel_grad.shape[1]))
+    scratch = [(4, 4), (4, 4), (3, 4), (4,), (3,)]
+    return small_sum(scatter_kernel, value, scratch, 7, 1, "scatter_sum")
+
+
+def along_sum(piece):
+    return small_sum(along_kernel, piece, [(4,), (2,), (2,)], 5, 2, "along_sum")
+
+
+def sums_kernel(
+    head_ref, returned_ref, rel_ref,
+    entity_grad, relation_grad,
+    mine, sent, far_up, far_down, both_up, both_down, got, shared,
+    whole,
+    send_sem, recv_sem,
+):
+    features, block = head_ref.shape
+    quarter = block // 4
+    region, x, y, z, core, peer, turn = position()
+    peers = [peer("core", 1), peer("r", 1), peer("r", 3)]
+    peers += [peer(a, s) for a in ("x", "y") for s in (1, 2, 3)]
+    greeted = greet(peers)
+
+    for q in range(4):
+        columns = slice(q * quarter, (q + 1) * quarter)
+        value = head_ref[:, columns] + returned_ref[:, columns].astype(F32)
+        mine[q] = value
+        sent[q] = value.astype(BF16)
+
+    greeted()
+    send = sender(send_sem, recv_sem)
+    steps = (2, 1, 3)
+    up, down, far = turn(region, 1), turn(region, 3), turn(region, 2)
+    above, below = peer("r", 1), peer("r", 3)
+    cut = far_up.shape[0]
+    top, low = pl.ds(0, cut), pl.ds(cut, features - cut)
+
+    far_copies = [
+        send(sent.at[far, top], far_up, above),
+        send(sent.at[far, low], far_down, below),
+    ]
+    near_copies = [
+        send(sent.at[up, low], got.at[0, low], above),
+        send(sent.at[down, top], got.at[1, top], below),
+    ]
+
+    whole[core, x, y] = rel_ref[...]
+    y_copies = [send(whole.at[core, x, y], whole.at[core, x, y], peer("y", s)) for s in steps]
 
     wait(far_copies)
     both_up[...] = (mine[up, :cut] + far_up[...].astype(F32)).astype(BF16)
@@ -238,10 +320,7 @@
     ]
 
     wait(y_copies)
-    lo_all[z] = x_sum[y] + y_got[0] + y_got[1] + y_got[2]
-    wait([send(lo_all.at[z], lo_all.at[z], peer("z", s)) for s in steps])
-    pair_mine[0] = lo_all[0] + lo_all[1] + lo_all[2] + lo_all[3]
-    pair_copies = [send(pair_mine.at[0], pair_got.at[0], first)]
+    x_copies = [send(whole.at[core, x], whole.at[core, x], peer("x", s)) for s in steps]
 
     wait(near_copies)
     total = mine[region] + got[0].astype(F32) + got[1].astype(F32)
@@ -255,19 +334,14 @@
         send(shared.at[region, top], shared.at[region, top], below),
     ]
 
-    wait(pair_copies)
-    pair_mine[1] = pair_mine[0] + pair_got[0]
-    pair_copies = [send(pair_mine.at[1], pair_got.at[1], second)]
+    wait(x_copies)
+    core_copies = [send(whole.at[core], whole.at[core], peer("core", 1))]
     wait(relayed)
     last_copies += [
         send(shared.at[down, top], shared.at[down, top], above),
         send(shared.at[up, low], shared.at[up, low], below),
     ]
-    wait(pair_copies)
-    whole[core, x, y] = pair_mine[1] + pair_got[1]
-    wait([send(whole.at[core, x, y], whole.at[core, x, y], peer("y", s)) for s in steps])
-    wait([send(whole.at[core, x], whole.at[core, x], peer("x", s)) for s in steps])
-    wait([send(whole.at[core], whole.at[core], peer("core", 1))])
+    wait(core_copies)
     for piece in range(features // 16):
         part = whole[piece // 16, piece // 4 % 4, piece % 4]
         relation_grad[piece * 16 : piece * 16 + 16, :] = part
@@ -277,13 +351,13 @@
         entity_grad[:, q * quarter : (q + 1) * quarter] = shared[q]
 
 
-def sum_all(head_grad, returned, rel_grad):
+def sum_all(head_grad, returned, rel_piece):
     features, block = head_grad.shape
-    rels = rel_grad.shape[1]
+    rels = rel_piece.shape[1]
     quarter = block // 4
     vmem = pl.BlockSpec(memory_space=pltpu.VMEM)
     piece = (16, rels)
-    copies = 31
+    copies = 19
     cut = (features // 2 + 15) // 16 * 16
     return pl.pallas_call(
         sums_kernel,
@@ -302,21 +376,13 @@
             pltpu.VMEM((features - cut, quarter), BF16),
             pltpu.VMEM((2, features, quarter), BF16),
             pltpu.VMEM((4, features, quarter), BF16),
-            pltpu.VMEM((4, 4) + piece, F32),
-            pltpu.VMEM((4, 4) + piece, F32),
-            pltpu.VMEM((3, 4) + piece, F32),
-            pltpu.VMEM((4,) + piece, F32),
-            pltpu.VMEM((3,) + piece, F32),
-            pltpu.VMEM((4,) + piece, F32),
-            pltpu.VMEM((2,) + piece, F32),
-            pltpu.VMEM((2,) + piece, F32),
             pltpu.VMEM((2, 4, 4) + piece, F32),
             pltpu.SemaphoreType.DMA((copies,)),
             pltpu.SemaphoreType.DMA((copies,)),
         ],
         compiler_params=pltpu.CompilerParams(collective_id=0, has_side_effects=True),
         name="sum_all",
-    )(head_grad, returned, rel_grad.reshape((2, 4, 4) + piece))
+    )(head_grad, returned, rel_piece)
 
 
 def shards(
@@ -334,8 +400,8 @@
         tail_index[None, :],
         negative_index,
     )
-    returned = route(partner_grad, pattern)
-    entity_grad, relation_grad = sum_all(head_grad, returned, rel_grad)
+    returned, rel_piece = route_beside(partner_grad, rel_grad, pattern)
+    entity_grad, relation_grad = sum_all(head_grad, returned, rel_piece)
     return entity - entity_rate * entity_grad.astype(F32), relation - relation_rate * relation_grad
 
 

time: 133 us -> 113 us (0.85)
  the two profiles are of different devices: /device:TPU:1 before, /device:TPU:9 now
where the time goes in v2:
time: 113 us; the launch traced here: 112 us
  Pallas kernels  79.9 us (71%)
  starting transfers between devices  17.8 us (16%)
  waiting for transfers between devices  8.13 us (7%)
  other arithmetic  4.08 us (4%)
  between operations  2 us (2%)
    pallas_call x1, Pallas kernels, sum_all(): pl.pallas_call(sums_kernel, out_shape=(jax.ShapeDtypeStruct((features, bl...  43.1 us
    pallas_call x2, Pallas kernels, small_sum(): pl.pallas_call(kernel, out_shape=jax.ShapeDtypeStruct(piece, F32), in_spe...  30 us
    ppermute x2, starting transfers between devices, move(): return lax.ppermute(value, ('region', 'dom'), pairs)  17.8 us
    ppermute x2, waiting for transfers between devices, move(): return lax.ppermute(value, ('region', 'dom'), pairs)  8.13 us
    pallas_call x1, Pallas kernels, edge_terms(): pl.pallas_call(terms_kernel, out_shape=(jax.ShapeDtypeStruct((features, b...  6.75 us
  transfers between devices with their start and end apart: 2, of which 1 were waited for; matrix products, arithmetic and copies ran while one was open for 0% of the time, Pallas kernels for 13%

profile of v2, /device:TPU:9, one launch (start us, length us, event | category | flops | bytes accessed | tf_op | source)
XLA Modules:
  0.0 112.3 jit_solution(3735951714004726774)
XLA Ops:
  1.9 1.2 %convert_element_type.30 = bf16[400,512]{1,0:T(8,128)(2,1)S(1)} convert(f32[400,512]{1,0:T(8,128)} %entity_ref.1) | non-fusion elementwise | flops 204800 | bytes 1228800 | tf_op jit(solution)/shard_map/convert_element_type | solution.py:392
  3.1 19.8 %conditional.4 = (bf16[400,512]{1,0:T(8,128)(2,1)S(1)}) conditional(s32[]{:T(128)} %bitcast.9, bf16[400,512]{1,0:T(8,128)(2,1)S(1)} %convert_element_type.30, bf16[400,512]{1,0:T(8,128)(2,1)S(1)} %convert_element_type.30, bf16[400,512]{1,0:T(8,128)(2,1)S(1)} %convert_element_type.30, ...), branch_computations={%region_0.0_spmd, %region_1.0_spmd, %region_2.0_spmd, %region_3.0_... | conditional | bytes 2457648 | solution.py:37
  3.2 11.6 %collective-permute-start.3 = (bf16[400,512]{1,0:T(8,128)(2,1)S(1)}, bf16[400,512]{1,0:T(8,128)(2,1)S(1)}, u32[]{:S(2)}, u32[]{:S(2)}) collective-permute-start(bf16[400,512]{1,0:T(8,128)(2,1)S(1)} %param.4), channel_id=1, source_target_pairs={{0,388},{1,389},{2,6},{3,7},{4,0},{5,1},{6,130},{7,131},{8,396},{9... | collective-permute-start | bytes 1228808 | tf_op jit(solution)/shard_map/cond/branch_4_fun/ppermute | solution.py:31
  14.7 8.1 %collective-permute-done.3 = bf16[400,512]{1,0:T(8,128)(2,1)S(1)} collective-permute-done((bf16[400,512]{1,0:T(8,128)(2,1)S(1)}, bf16[400,512]{1,0:T(8,128)(2,1)S(1)}, u32[]{:S(2)}, u32[]{:S(2)}) %collective-permute-start.3) | collective-permute-done | bytes 409632 | tf_op jit(solution)/shard_map/cond/branch_4_fun/ppermute | solution.py:31
  23.0 6.7 %edge_terms.1 = (f32[400,512]{1,0:T(8,128)}, bf16[400,512]{1,0:T(8,128)(2,1)S(1)}, f32[512,256]{1,0:T(8,128)S(1)}) custom-call(s32[1]{0:T(128)S(6)} %copy.83.count_ref, f32[400,512]{1,0:T(8,128)} %entity_ref.1, f32[400,256]{1,0:T(8,128)} %relation_ref.1, bf16[400,512]{1,0:T(8,128)(2,1)S(1)} %get-tuple-element.263.partner_ref, s32[1,512]{1,0:T(1,128)} %bitcast.21, ...), custom_call_target="tpu_custom_call" | custom-call | tf_op jit(solution)/shard_map/edge_terms/pallas_call | solution.py:142
  29.7 21.2 %conditional.6 = (bf16[400,512]{1,0:T(8,128)(2,1)S(1)}, f32[16,256]{1,0:T(8,128)S(1)}) conditional(s32[]{:T(128)} %bitcast.9, (f32[512,256]{1,0:T(8,128)S(1)}, bf16[400,512]{1,0:T(8,128)(2,1)S(1)}) %tuple.161, (bf16[400,512]{1,0:T(8,128)(2,1)S(1)}, f32[512,256]{1,0:T(8,128)S(1)}) %tuple.162, ...), branch_computations={%region_24.0_spmd, %region_25.0_spmd, %region_26.0_spmd, %region_2... | conditional | flops 10000000 | bytes 12457656 | solution.py:50
  29.7 6.2 %collective-permute-start.25 = (bf16[400,512]{1,0:T(8,128)(2,1)S(1)}, bf16[400,512]{1,0:T(8,128)(2,1)S(1)}, u32[]{:S(2)}, u32[]{:S(2)}) collective-permute-start(bf16[400,512]{1,0:T(8,128)(2,1)S(1)} %get-tuple-element.154), channel_id=1, source_target_pairs={{0,388},{1,389},{2,6},{3,7},{4,0},{5,1},{6,130},{7,131},{8,396},{9... | collective-permute-start | bytes 1228808 | tf_op jit(solution)/shard_map/cond/branch_4_fun/ppermute | solution.py:31
  35.9 15.0 %scatter_sum.12 = f32[16,256]{1,0:T(8,128)S(1)} custom-call(f32[2,4,4,16,256]{4,3,2,1,0:T(8,128)S(1)} %bitcast.17), custom_call_target="tpu_custom_call" | custom-call | flops 10000000 | bytes 10000000 | tf_op jit(solution)/shard_map/cond/branch_4_fun/scatter_sum/pallas_call | solution.py:251
  50.9 0.0 collective-permute-done.25
  51.0 15.3 %conditional.7 = (bf16[400,512]{1,0:T(8,128)(2,1)S(1)}, f32[16,256]{1,0:T(8,128)S(1)}) conditional(s32[]{:T(128)} %bitcast.8, (f32[16,256]{1,0:T(8,128)S(1)}, bf16[400,512]{1,0:T(8,128)(2,1)S(1)}) %tuple.163, (bf16[400,512]{1,0:T(8,128)(2,1)S(1)}, f32[16,256]{1,0:T(8,128)S(1)}) %conditional.6, ...), branch_computations={%region_32.0_spmd, %region_33.0_spmd, %region_34.0_spmd, %region_3... | conditional | flops 10000000 | bytes 12457656 | solution.py:51
  51.0 15.0 %along_sum.16 = f32[16,256]{1,0:T(8,128)S(1)} custom-call(f32[16,256]{1,0:T(8,128)S(1)} %get-tuple-element.163.piece_ref), custom_call_target="tpu_custom_call" | custom-call | flops 10000000 | bytes 10000000 | tf_op jit(solution)/shard_map/cond/branch_0_fun/along_sum/pallas_call | solution.py:251
  66.2 0.0 copy-start
  66.2 43.1 %sum_all.1 = (bf16[400,512]{1,0:T(8,128)(2,1)}, f32[400,256]{1,0:T(8,128)}) custom-call(f32[400,512]{1,0:T(8,128)} %get-tuple-element.205.head_ref, bf16[400,512]{1,0:T(8,128)(2,1)S(1)} %get-tuple-element.210.returned_ref, f32[16,256]{1,0:T(8,128)S(1)} %get-tuple-element.211.rel_ref), custom_call_target="tpu_custom_call" | custom-call | tf_op jit(solution)/shard_map/sum_all/pallas_call | solution.py:362
  109.4 0.0 copy-done
  109.4 0.0 copy-start.1
  109.4 0.0 copy-start.2
  109.4 2.1 %convert_subtract_fusion = f32[400,512]{1,0:T(8,128)} fusion(f32[400,512]{1,0:T(8,128)S(1)} %copy-done, bf16[400,512]{1,0:T(8,128)(2,1)} %get-tuple-element.212), kind=kLoop, calls=%fused_computation | loop fusion | flops 409600 | bytes 2048000 | tf_op jit(solution)/shard_map/sub | solution.py:405
  111.5 0.0 copy-done.1
  111.5 0.0 copy-done.2
  111.5 0.8 multiply_subtract_fusion
  (3 shorter events, 0.1 us)
Async XLA Ops:
  3.2 19.7 %collective-permute-start.3 = (bf16[400,512]{1,0:T(8,128)(2,1)S(1)}, bf16[400,512]{1,0:T(8,128)(2,1)S(1)}, u32[]{:S(2)}, u32[]{:S(2)}) collective-permute-start(bf16[400,512]{1,0:T(8,128)(2,1)S(1)} %param.4), channel_id=1, source_target_pairs={{0,388},{1,389},{2,6},{3,7},{4,0},{5,1},{6,130},{7,131},{8,396},{9... | collective-permute-start | bytes 1228808 | tf_op jit(solution)/shard_map/cond/branch_4_fun/ppermute | solution.py:31
  29.7 21.2 %collective-permute-start.25 = (bf16[400,512]{1,0:T(8,128)(2,1)S(1)}, bf16[400,512]{1,0:T(8,128)(2,1)S(1)}, u32[]{:S(2)}, u32[]{:S(2)}) collective-permute-start(bf16[400,512]{1,0:T(8,128)(2,1)S(1)} %get-tuple-element.154), channel_id=1, source_target_pairs={{0,388},{1,389},{2,6},{3,7},{4,0},{5,1},{6,130},{7,131},{8,396},{9... | collective-permute-start | bytes 1228808 | tf_op jit(solution)/shard_map/cond/branch_4_fun/ppermute | solution.py:31
  66.2 43.1 %copy-start = (f32[400,512]{1,0:T(8,128)S(1)}, f32[400,512]{1,0:T(8,128)}, u32[]{:S(2)}) copy-start(f32[400,512]{1,0:T(8,128)} %entity_ref.1) | copy-start | bytes 2457604
  109.4 2.1 %copy-start.1 = (f32[400,256]{1,0:T(8,128)S(1)}, f32[400,256]{1,0:T(8,128)}, u32[]{:S(2)}) copy-start(f32[400,256]{1,0:T(8,128)} %relation_ref.1) | copy-start | bytes 1228804
  109.4 2.1 %copy-start.2 = (f32[400,256]{1,0:T(8,128)S(1)}, f32[400,256]{1,0:T(8,128)}, u32[]{:S(2)}) copy-start(f32[400,256]{1,0:T(8,128)} %get-tuple-element.213) | copy-start | bytes 1228804

commit v3 on v2

--- a/solution.py
+++ b/solution.py
@@ -231,18 +231,14 @@
     piece_ref[...] = x_sum[y] + y_got[0] + y_got[1] + y_got[2]
 
 
-def along_kernel(piece_ref, sum_ref, lo_all, pair_mine, pair_got, send_sem, recv_sem):
+def along_kernel(piece_ref, sum_ref, lo_all, send_sem, recv_sem):
     region, x, y, z, core, peer, turn = position()
     steps = (2, 1, 3)
-    greet([peer("z", s) for s in steps] + [peer("r", 1), peer("r", 3)])()
+    greet([peer("z", s) for s in steps])()
     send = sender(send_sem, recv_sem)
     lo_all[z] = piece_ref[...]
     wait([send(lo_all.at[z], lo_all.at[z], peer("z", s)) for s in steps])
-    pair_mine[0] = lo_all[0] + lo_all[1] + lo_all[2] + lo_all[3]
-    wait([send(pair_mine.at[0], pair_got.at[0], peer("pair", 1))])
-    pair_mine[1] = pair_mine[0] + pair_got[0]
-    wait([send(pair_mine.at[1], pair_got.at[1], peer("pair", 2))])
-    sum_ref[...] = pair_mine[1] + pair_got[1]
+    sum_ref[...] = lo_all[0] + lo_all[1] + lo_all[2] + lo_all[3]
 
 
 def small_sum(kernel, value, scratch, copies, number, name):
@@ -268,14 +264,14 @@
 
 
 def along_sum(piece):
-    return small_sum(along_kernel, piece, [(4,), (2,), (2,)], 5, 2, "along_sum")
+    return small_sum(along_kernel, piece, [(4,)], 3, 2, "along_sum")
 
 
 def sums_kernel(
     head_ref, returned_ref, rel_ref,
     entity_grad, relation_grad,
     mine, sent, far_up, far_down, both_up, both_down, got, shared,
-    whole,
+    pair_mine, pair_got, whole,
     send_sem, recv_sem,
 ):
     features, block = head_ref.shape
@@ -299,6 +295,8 @@
     cut = far_up.shape[0]
     top, low = pl.ds(0, cut), pl.ds(cut, features - cut)
 
+    pair_mine[0] = rel_ref[...]
+    pair_copies = [send(pair_mine.at[0], pair_got.at[0], peer("pair", 1))]
     far_copies = [
         send(sent.at[far, top], far_up, above),
         send(sent.at[far, low], far_down, below),
@@ -308,8 +306,9 @@
         send(sent.at[down, top], got.at[1, top], below),
     ]
 
-    whole[core, x, y] = rel_ref[...]
-    y_copies = [send(whole.at[core, x, y], whole.at[core, x, y], peer("y", s)) for s in steps]
+    wait(pair_copies)
+    pair_mine[1] = pair_mine[0] + pair_got[0]
+    pair_copies = [send(pair_mine.at[1], pair_got.at[1], peer("pair", 2))]
 
     wait(far_copies)
     both_up[...] = (mine[up, :cut] + far_up[...].astype(F32)).astype(BF16)
@@ -319,8 +318,9 @@
         send(both_down, got.at[1, low], below),
     ]
 
-    wait(y_copies)
-    x_copies = [send(whole.at[core, x], whole.at[core, x], peer("x", s)) for s in steps]
+    wait(pair_copies)
+    whole[core, x, y] = pair_mine[1] + pair_got[1]
+    y_copies = [send(whole.at[core, x, y], whole.at[core, x, y], peer("y", s)) for s in steps]
 
     wait(near_copies)
     total = mine[region] + got[0].astype(F32) + got[1].astype(F32)
@@ -333,6 +333,8 @@
         send(shared.at[region, low], shared.at[region, low], above),
         send(shared.at[region, top], shared.at[region, top], below),
     ]
+    wait(y_copies)
+    x_copies = [send(whole.at[core, x], whole.at[core, x], peer("x", s)) for s in steps]
 
     wait(x_copies)
     core_copies = [send(whole.at[core], whole.at[core], peer("core", 1))]
@@ -357,7 +359,7 @@
     quarter = block // 4
     vmem = pl.BlockSpec(memory_space=pltpu.VMEM)
     piece = (16, rels)
-    copies = 19
+    copies = 21
     cut = (features // 2 + 15) // 16 * 16
     return pl.pallas_call(
         sums_kernel,
@@ -376,6 +378,8 @@
             pltpu.VMEM((features - cut, quarter), BF16),
             pltpu.VMEM((2, features, quarter), BF16),
             pltpu.VMEM((4, features, quarter), BF16),
+            pltpu.VMEM((2,) + piece, F32),
+            pltpu.VMEM((2,) + piece, F32),
             pltpu.VMEM((2, 4, 4) + piece, F32),
             pltpu.SemaphoreType.DMA((copies,)),
             pltpu.SemaphoreType.DMA((copies,)),

time: 113 us -> 125 us (1.11)
  the two profiles are of different devices: /device:TPU:9 before, /device:TPU:1 now
where the time goes in v3:
time: 125 us; the launch traced here: 122 us
  Pallas kernels  71.5 us (57%)
  starting transfers between devices  24.4 us (20%)
  waiting for transfers between devices  19.7 us (16%)
  other arithmetic  4.08 us (3%)
  between operations  2 us (2%)
    pallas_call x1, Pallas kernels, sum_all(): pl.pallas_call(sums_kernel, out_shape=(jax.ShapeDtypeStruct((features, bl...  43 us
    ppermute x4, starting transfers between devices, move(): return lax.ppermute(value, ('region', 'dom'), pairs)  24.4 us
    pallas_call x2, Pallas kernels, small_sum(): pl.pallas_call(kernel, out_shape=jax.ShapeDtypeStruct(piece, F32), in_spe...  21.8 us
    ppermute x4, waiting for transfers between devices, move(): return lax.ppermute(value, ('region', 'dom'), pairs)  19.7 us
    pallas_call x1, Pallas kernels, edge_terms(): pl.pallas_call(terms_kernel, out_shape=(jax.ShapeDtypeStruct((features, b...  6.75 us
  transfers between devices with their start and end apart: 4, of which 3 were waited for; matrix products, arithmetic and copies ran while one was open for 0% of the time, Pallas kernels for 18%

profile of v3, /device:TPU:1, one launch (start us, length us, event | category | flops | bytes accessed | tf_op | source)
XLA Modules:
  0.0 122.1 jit_solution(8267670164402230745)
XLA Ops:
  1.9 1.2 convert_element_type.30
  3.1 20.6 %conditional.4 = (bf16[400,512]{1,0:T(8,128)(2,1)S(1)}) conditional(s32[]{:T(128)} %bitcast.9, bf16[400,512]{1,0:T(8,128)(2,1)S(1)} %convert_element_type.30, bf16[400,512]{1,0:T(8,128)(2,1)S(1)} %convert_element_type.30, bf16[400,512]{1,0:T(8,128)(2,1)S(1)} %convert_element_type.30, ...), branch_computations={%region_0.0_spmd, %region_1.0_spmd, %region_2.0_spmd, %region_3.0_... | conditional | bytes 2457648 | solution.py:37
  3.2 12.4 %collective-permute-start.3 = (bf16[400,512]{1,0:T(8,128)(2,1)S(1)}, bf16[400,512]{1,0:T(8,128)(2,1)S(1)}, u32[]{:S(2)}, u32[]{:S(2)}) collective-permute-start(bf16[400,512]{1,0:T(8,128)(2,1)S(1)} %param.4), channel_id=1, source_target_pairs={{0,388},{1,389},{2,6},{3,7},{4,0},{5,1},{6,130},{7,131},{8,396},{9... | collective-permute-start | bytes 1228808 | tf_op jit(solution)/shard_map/cond/branch_4_fun/ppermute | solution.py:31
  15.6 8.1 %collective-permute-done.3 = bf16[400,512]{1,0:T(8,128)(2,1)S(1)} collective-permute-done((bf16[400,512]{1,0:T(8,128)(2,1)S(1)}, bf16[400,512]{1,0:T(8,128)(2,1)S(1)}, u32[]{:S(2)}, u32[]{:S(2)}) %collective-permute-start.3) | collective-permute-done | bytes 409632 | tf_op jit(solution)/shard_map/cond/branch_4_fun/ppermute | solution.py:31
  23.7 11.5 %conditional.5 = (bf16[400,512]{1,0:T(8,128)(2,1)S(1)}) conditional(s32[]{:T(128)} %bitcast.8, bf16[400,512]{1,0:T(8,128)(2,1)S(1)} %get-tuple-element.262, bf16[400,512]{1,0:T(8,128)(2,1)S(1)} %get-tuple-element.262, bf16[400,512]{1,0:T(8,128)(2,1)S(1)} %get-tuple-element.262, ...), branch_computations={%region_8.0_spmd, %region_9.0_spmd, %region_10.0_spmd, %region_11.... | conditional | bytes 2457648 | solution.py:38
  23.8 3.2 %collective-permute-start.7 = (bf16[400,512]{1,0:T(8,128)(2,1)S(1)}, bf16[400,512]{1,0:T(8,128)(2,1)S(1)}, u32[]{:S(2)}, u32[]{:S(2)}) collective-permute-start(bf16[400,512]{1,0:T(8,128)(2,1)S(1)} %param.9), channel_id=1, source_target_pairs={{0,8},{1,9},{2,10},{3,11},{4,12},{5,13},{6,14},{7,15},{8,0},{9,1},... | collective-permute-start | bytes 1228808 | tf_op jit(solution)/shard_map/cond/branch_1_fun/ppermute | solution.py:31
  27.0 8.2 %collective-permute-done.7 = bf16[400,512]{1,0:T(8,128)(2,1)S(1)} collective-permute-done((bf16[400,512]{1,0:T(8,128)(2,1)S(1)}, bf16[400,512]{1,0:T(8,128)(2,1)S(1)}, u32[]{:S(2)}, u32[]{:S(2)}) %collective-permute-start.7) | collective-permute-done | bytes 409632 | tf_op jit(solution)/shard_map/cond/branch_1_fun/ppermute | solution.py:31
  35.2 6.7 %edge_terms.1 = (f32[400,512]{1,0:T(8,128)}, bf16[400,512]{1,0:T(8,128)(2,1)S(1)}, f32[512,256]{1,0:T(8,128)S(1)}) custom-call(s32[1]{0:T(128)S(6)} %copy.83.count_ref, f32[400,512]{1,0:T(8,128)} %entity_ref.1, f32[400,256]{1,0:T(8,128)} %relation_ref.1, bf16[400,512]{1,0:T(8,128)(2,1)S(1)} %get-tuple-element.263.partner_ref, s32[1,512]{1,0:T(1,128)} %bitcast.21, ...), custom_call_target="tpu_custom_call" | custom-call | tf_op jit(solution)/shard_map/edge_terms/pallas_call | solution.py:142
  42.0 22.7 %conditional.6 = (bf16[400,512]{1,0:T(8,128)(2,1)S(1)}, f32[16,256]{1,0:T(8,128)S(1)}) conditional(s32[]{:T(128)} %bitcast.9, (f32[512,256]{1,0:T(8,128)S(1)}, bf16[400,512]{1,0:T(8,128)(2,1)S(1)}) %tuple.161, (bf16[400,512]{1,0:T(8,128)(2,1)S(1)}, f32[512,256]{1,0:T(8,128)S(1)}) %tuple.162, ...), branch_computations={%region_24.0_spmd, %region_25.0_spmd, %region_26.0_spmd, %region_2... | conditional | flops 10000000 | bytes 12457656 | solution.py:50
  42.0 6.2 %collective-permute-start.25 = (bf16[400,512]{1,0:T(8,128)(2,1)S(1)}, bf16[400,512]{1,0:T(8,128)(2,1)S(1)}, u32[]{:S(2)}, u32[]{:S(2)}) collective-permute-start(bf16[400,512]{1,0:T(8,128)(2,1)S(1)} %get-tuple-element.154), channel_id=1, source_target_pairs={{0,388},{1,389},{2,6},{3,7},{4,0},{5,1},{6,130},{7,131},{8,396},{9... | collective-permute-start | bytes 1228808 | tf_op jit(solution)/shard_map/cond/branch_4_fun/ppermute | solution.py:31
  48.2 16.4 %scatter_sum.12 = f32[16,256]{1,0:T(8,128)S(1)} custom-call(f32[2,4,4,16,256]{4,3,2,1,0:T(8,128)S(1)} %bitcast.17), custom_call_target="tpu_custom_call" | custom-call | flops 10000000 | bytes 10000000 | tf_op jit(solution)/shard_map/cond/branch_4_fun/scatter_sum/pallas_call | solution.py:247
  64.5 0.0 collective-permute-done.25
  64.6 11.5 %conditional.7 = (bf16[400,512]{1,0:T(8,128)(2,1)S(1)}, f32[16,256]{1,0:T(8,128)S(1)}) conditional(s32[]{:T(128)} %bitcast.8, (f32[16,256]{1,0:T(8,128)S(1)}, bf16[400,512]{1,0:T(8,128)(2,1)S(1)}) %tuple.163, (bf16[400,512]{1,0:T(8,128)(2,1)S(1)}, f32[16,256]{1,0:T(8,128)S(1)}) %conditional.6, ...), branch_computations={%region_32.0_spmd, %region_33.0_spmd, %region_34.0_spmd, %region_3... | conditional | flops 10000000 | bytes 12457656 | solution.py:51
  64.6 2.6 %collective-permute-start.29 = (bf16[400,512]{1,0:T(8,128)(2,1)S(1)}, bf16[400,512]{1,0:T(8,128)(2,1)S(1)}, u32[]{:S(2)}, u32[]{:S(2)}) collective-permute-start(bf16[400,512]{1,0:T(8,128)(2,1)S(1)} %get-tuple-element.164), channel_id=1, source_target_pairs={{0,8},{1,9},{2,10},{3,11},{4,12},{5,13},{6,14},{7,15},{8,0},{9,1},... | collective-permute-start | bytes 1228808 | tf_op jit(solution)/shard_map/cond/branch_1_fun/ppermute | solution.py:31
  67.3 5.4 %along_sum.17 = f32[16,256]{1,0:T(8,128)S(1)} custom-call(f32[16,256]{1,0:T(8,128)S(1)} %get-tuple-element.165.piece_ref), custom_call_target="tpu_custom_call" | custom-call | flops 10000000 | bytes 10000000 | tf_op jit(solution)/shard_map/cond/branch_1_fun/along_sum/pallas_call | solution.py:247
  72.7 3.4 %collective-permute-done.29 = bf16[400,512]{1,0:T(8,128)(2,1)S(1)} collective-permute-done((bf16[400,512]{1,0:T(8,128)(2,1)S(1)}, bf16[400,512]{1,0:T(8,128)(2,1)S(1)}, u32[]{:S(2)}, u32[]{:S(2)}) %collective-permute-start.29) | collective-permute-done | bytes 409632 | tf_op jit(solution)/shard_map/cond/branch_1_fun/ppermute | solution.py:31
  76.1 0.0 copy-start
  76.2 43.0 %sum_all.1 = (bf16[400,512]{1,0:T(8,128)(2,1)}, f32[400,256]{1,0:T(8,128)}) custom-call(f32[400,512]{1,0:T(8,128)} %get-tuple-element.205.head_ref, bf16[400,512]{1,0:T(8,128)(2,1)S(1)} %get-tuple-element.210.returned_ref, f32[16,256]{1,0:T(8,128)S(1)} %get-tuple-element.211.rel_ref), custom_call_target="tpu_custom_call" | custom-call | tf_op jit(solution)/shard_map/sum_all/pallas_call | solution.py:364
  119.1 0.0 copy-done
  119.1 0.0 copy-start.1
  119.2 0.0 copy-start.2
  119.2 2.1 %convert_subtract_fusion = f32[400,512]{1,0:T(8,128)} fusion(f32[400,512]{1,0:T(8,128)S(1)} %copy-done, bf16[400,512]{1,0:T(8,128)(2,1)} %get-tuple-element.212), kind=kLoop, calls=%fused_computation | loop fusion | flops 409600 | bytes 2048000 | tf_op jit(solution)/shard_map/sub | solution.py:409
  121.2 0.0 copy-done.1
  121.3 0.8 multiply_subtract_fusion
  (5 shorter events, 0.1 us)
Async XLA Ops:
  3.2 20.5 %collective-permute-start.3 = (bf16[400,512]{1,0:T(8,128)(2,1)S(1)}, bf16[400,512]{1,0:T(8,128)(2,1)S(1)}, u32[]{:S(2)}, u32[]{:S(2)}) collective-permute-start(bf16[400,512]{1,0:T(8,128)(2,1)S(1)} %param.4), channel_id=1, source_target_pairs={{0,388},{1,389},{2,6},{3,7},{4,0},{5,1},{6,130},{7,131},{8,396},{9... | collective-permute-start | bytes 1228808 | tf_op jit(solution)/shard_map/cond/branch_4_fun/ppermute | solution.py:31
  23.8 11.4 %collective-permute-start.7 = (bf16[400,512]{1,0:T(8,128)(2,1)S(1)}, bf16[400,512]{1,0:T(8,128)(2,1)S(1)}, u32[]{:S(2)}, u32[]{:S(2)}) collective-permute-start(bf16[400,512]{1,0:T(8,128)(2,1)S(1)} %param.9), channel_id=1, source_target_pairs={{0,8},{1,9},{2,10},{3,11},{4,12},{5,13},{6,14},{7,15},{8,0},{9,1},... | collective-permute-start | bytes 1228808 | tf_op jit(solution)/shard_map/cond/branch_1_fun/ppermute | solution.py:31
  42.0 22.6 %collective-permute-start.25 = (bf16[400,512]{1,0:T(8,128)(2,1)S(1)}, bf16[400,512]{1,0:T(8,128)(2,1)S(1)}, u32[]{:S(2)}, u32[]{:S(2)}) collective-permute-start(bf16[400,512]{1,0:T(8,128)(2,1)S(1)} %get-tuple-element.154), channel_id=1, source_target_pairs={{0,388},{1,389},{2,6},{3,7},{4,0},{5,1},{6,130},{7,131},{8,396},{9... | collective-permute-start | bytes 1228808 | tf_op jit(solution)/shard_map/cond/branch_4_fun/ppermute | solution.py:31
  64.6 11.4 %collective-permute-start.29 = (bf16[400,512]{1,0:T(8,128)(2,1)S(1)}, bf16[400,512]{1,0:T(8,128)(2,1)S(1)}, u32[]{:S(2)}, u32[]{:S(2)}) collective-permute-start(bf16[400,512]{1,0:T(8,128)(2,1)S(1)} %get-tuple-element.164), channel_id=1, source_target_pairs={{0,8},{1,9},{2,10},{3,11},{4,12},{5,13},{6,14},{7,15},{8,0},{9,1},... | collective-permute-start | bytes 1228808 | tf_op jit(solution)/shard_map/cond/branch_1_fun/ppermute | solution.py:31
  76.1 43.0 %copy-start = (f32[400,512]{1,0:T(8,128)S(1)}, f32[400,512]{1,0:T(8,128)}, u32[]{:S(2)}) copy-start(f32[400,512]{1,0:T(8,128)} %entity_ref.1) | copy-start | bytes 2457604
  119.1 2.1 %copy-start.1 = (f32[400,256]{1,0:T(8,128)S(1)}, f32[400,256]{1,0:T(8,128)}, u32[]{:S(2)}) copy-start(f32[400,256]{1,0:T(8,128)} %relation_ref.1) | copy-start | bytes 1228804
  119.2 2.1 %copy-start.2 = (f32[400,256]{1,0:T(8,128)S(1)}, f32[400,256]{1,0:T(8,128)}, u32[]{:S(2)}) copy-start(f32[400,256]{1,0:T(8,128)} %get-tuple-element.213) | copy-start | bytes 1228804
